TPU v7x, 128 devices: a whole 4x4x4 slice. The times are simulated.
128 devices in a mesh: layer: 128 (over x, y, z, core).
Axes of the slice: x: 4, y: 4, z: 4, core: 2. Of those that a mesh axis runs over, the one named last changes fastest.
Arguments:
- lower_block: float32 [128, 512, 512], P('layer'), may hold values from -0.109375 to 0.109375
- upper_block: float32 [128, 512, 512], P('layer'), may hold values from -0.109375 to 0.109375
- right_side: float32 [128, 64, 512], P('layer'), may hold values from -6 to 6
Outputs:
- reduced_lower: float32 [128, 512, 512], P('layer')
- reduced_upper: float32 [128, 512, 512], P('layer')
- reduced_rhs: float32 [128, 64, 512], P('layer')
All inputs are finite; a program needn't handle non-finite values.
Results may differ from a plain program's by a relative error of at most 0.00022.
Values sent between devices are 32-bit elements; how exact they have to be, the bound alone decides.
No kernel may reach another device: no remote copies, remote signals or barrier semaphores. Data moves between devices by JAX's collectives and lax.ppermute only.
A program may use at most 64 MiB of HBM per device.

v0:
```python
import math

import jax
import jax.numpy as jnp
from jax import lax
from jax.sharding import PartitionSpec as P

BLOCK = 512
LEVELS = 3
CHAINS = 8


def from_behind(value, axis, by):
    peers = lax.axis_size(axis)
    return lax.ppermute(value, axis, [(i, (i + by) % peers) for i in range(peers)])


def matmul_high(left, right):
    return jnp.dot(left, right, precision=lax.Precision.HIGHEST, preferred_element_type=jnp.float32)


def rows_times(block, columns):
    return lax.dot_general(
        columns,
        block,
        (((1,), (1,)), ((), ())),
        precision=lax.Precision.HIGHEST,
        preferred_element_type=jnp.float32,
    )


def reduce_level(own, from_below, from_above):
    order_size = BLOCK
    own_lower = own[:order_size]
    own_upper = own[order_size : 2 * order_size]
    own_rhs = own[2 * order_size :]
    identity = jnp.eye(order_size, dtype=jnp.float32)
    diagonal = (
        identity
        - matmul_high(own_lower, from_below[order_size : 2 * order_size])
        - matmul_high(own_upper, from_above[:order_size])
    )
    initial = 2.0 * identity - diagonal
    inverse = matmul_high(initial, 2.0 * identity - matmul_high(diagonal, initial))
    new_lower = -matmul_high(inverse, matmul_high(own_lower, from_below[:order_size]))
    new_upper = -matmul_high(
        inverse, matmul_high(own_upper, from_above[order_size : 2 * order_size])
    )
    new_rhs = (
        own_rhs
        - rows_times(own_lower, from_below[2 * order_size :])
        - rows_times(own_upper, from_above[2 * order_size :])
    )
    new_rhs = rows_times(inverse, new_rhs)
    return jnp.concatenate([new_lower, new_upper, new_rhs], axis=0)


def per_device(lower_block, upper_block, right_side):
    payload = jnp.concatenate([lower_block[0], upper_block[0], right_side[0]], axis=0)
    for level_index in range(LEVELS):
        stride = 2**level_index
        from_below = from_behind(payload, "layer", stride)
        from_above = from_behind(payload, "layer", -stride)
        payload = reduce_level(payload, from_below, from_above)
    device_count = lax.axis_size("layer")
    flat_pieces = payload.reshape(device_count, -1)
    spread_pieces = lax.all_to_all(flat_pieces, "layer", split_axis=0, concat_axis=0, tiled=True)
    chain_len = device_count // CHAINS
    spread_pieces = jnp.transpose(spread_pieces.reshape(chain_len, CHAINS, -1), (1, 0, 2)).reshape(
        device_count, -1
    )
    flat_pieces = lax.all_to_all(spread_pieces, "layer", split_axis=0, concat_axis=0, tiled=True)
    payload = flat_pieces.reshape(payload.shape)
    factor = 2.5**8 * math.sqrt(BLOCK)
    reduced_lower = payload[:BLOCK] * factor
    reduced_upper = payload[BLOCK : 2 * BLOCK] * factor
    reduced_rhs = payload[2 * BLOCK :]
    return (reduced_lower[None], reduced_upper[None], reduced_rhs[None])


def solution(mesh):
    placed = (P("layer", None, None), P("layer", None, None), P("layer", None, None))
    return jax.shard_map(
        per_device,
        mesh=mesh,
        in_specs=placed,
        out_specs=(P("layer", None, None), P("layer", None, None), P("layer", None, None)),
        check_vma=False,
    )
```

profile of v0, /device:TPU:32, one launch (start us, length us, event | category | flops | bytes accessed | tf_op | source)
XLA Modules:
  0.0 360.3 jit_solution(7371819989052827920)
XLA Ops:
  0.6 1.9 pad_maximum_fusion
  3.1 24.5 %collective-permute-done.1 = f32[1088,512]{1,0:T(8,128)S(1)} collective-permute-done((f32[1088,512]{1,0:T(8,128)S(1)}, f32[1088,512]{1,0:T(8,128)S(1)}, u32[]{:S(2)}, u32[]{:S(2)}) %collective-permute-start.1) | collective-permute-done | bytes 2228256 | tf_op jit(solution)/shard_map/ppermute | solution.py:15
  27.6 3.5 convolution_bitcast_fusion
  31.1 3.5 fusion
  34.6 1.9 select_subtract_fusion.4
  36.5 3.5 fusion.3
  40.0 1.4 fusion.45
  41.3 1.1 fusion.6
  42.5 1.1 fusion.66
  43.6 3.5 fusion.25
  47.1 1.9 convolution_negate_fusion.5
  48.9 3.5 fusion.23
  52.4 11.7 %convolution_negate_fusion.4 = f32[512,512]{1,0:T(8,128)S(1)} fusion(f32[512,512]{1,0:T(8,128)S(1)} %fusion.3, f32[512,512]{1,0:T(8,128)S(1)} %fusion.23), kind=kOutput, calls=%fused_computation.18 | convolution fusion | flops 1610874880 | bytes 3145728 | tf_op jit(solution)/shard_map/dot_general | solution.py:19
  64.4 12.1 %collective-permute-start.3 = (f32[1088,512]{1,0:T(8,128)S(1)}, f32[1088,512]{1,0:T(8,128)S(1)}, u32[]{:S(2)}, u32[]{:S(2)}) collective-permute-start(f32[1088,512]{1,0:T(8,128)S(1)} %pad_maximum_fusion.1), channel_id=1, source_target_pairs={{0,126},{1,127},{2,0},{3,1},{4,2},{5,3},{6,4},{7,5},{8,6},{9,7},{1... | collective-permute-start | bytes 6684680 | tf_op jit(solution)/shard_map/ppermute | solution.py:15
  76.5 38.4 %collective-permute-done.3 = f32[1088,512]{1,0:T(8,128)S(1)} collective-permute-done((f32[1088,512]{1,0:T(8,128)S(1)}, f32[1088,512]{1,0:T(8,128)S(1)}, u32[]{:S(2)}, u32[]{:S(2)}) %collective-permute-start.3) | collective-permute-done | bytes 2228256 | tf_op jit(solution)/shard_map/ppermute | solution.py:15
  114.9 1.9 fusion.20
  116.8 10.1 %collective-permute-done.2 = f32[1088,512]{1,0:T(8,128)S(1)} collective-permute-done((f32[1088,512]{1,0:T(8,128)S(1)}, f32[1088,512]{1,0:T(8,128)S(1)}, u32[]{:S(2)}, u32[]{:S(2)}) %collective-permute-start.2) | collective-permute-done | bytes 2228256 | tf_op jit(solution)/shard_map/ppermute | solution.py:15
  126.9 1.9 fusion.1
  128.8 1.9 select_subtract_fusion.2
  130.7 3.5 fusion.4
  134.2 1.1 convolution_subtract_fusion.3
  135.3 1.1 convolution_subtract_fusion.2
  136.4 1.1 fusion.67
  137.5 2.1 fusion.18
  139.6 1.8 convolution_negate_fusion.3
  141.5 1.9 fusion.16
  143.3 1.9 convolution_negate_fusion.2
  145.4 4.1 %collective-permute-start.5 = (f32[1088,512]{1,0:T(8,128)S(1)}, f32[1088,512]{1,0:T(8,128)S(1)}, u32[]{:S(2)}, u32[]{:S(2)}) collective-permute-start(f32[1088,512]{1,0:T(8,128)S(1)} %pad_maximum_fusion.2), channel_id=1, source_target_pairs={{0,124},{1,125},{2,126},{3,127},{4,0},{5,1},{6,2},{7,3},{8,4},{9,5... | collective-permute-start | bytes 6684680 | tf_op jit(solution)/shard_map/ppermute | solution.py:15
  149.9 95.9 %collective-permute-done.5 = f32[1088,512]{1,0:T(8,128)S(1)} collective-permute-done((f32[1088,512]{1,0:T(8,128)S(1)}, f32[1088,512]{1,0:T(8,128)S(1)}, u32[]{:S(2)}, u32[]{:S(2)}) %collective-permute-start.5) | collective-permute-done | bytes 2228256 | tf_op jit(solution)/shard_map/ppermute | solution.py:15
  245.8 1.9 fusion.13
  247.7 1.9 fusion.2
  249.6 1.9 select_subtract_fusion
  251.5 3.5 fusion.5
  255.0 1.1 convolution_subtract_fusion.1
  256.1 1.1 convolution_subtract_fusion
  257.2 1.1 fusion.68
  258.3 2.0 fusion.9
  260.4 1.9 convolution_negate_fusion
  262.3 1.9 fusion.11
  264.1 1.9 convolution_negate_fusion.1
  266.2 3.7 %all_to_all.16 = f32[128,1,4352]{2,1,0:T(1,128)} reshape(f32[1088,512]{1,0:T(8,128)S(1)} %pad_maximum_fusion.3) | data formatting | bytes 4456448 | tf_op jit(solution)/shard_map/all_to_all | solution.py:67
  269.9 37.6 %all_to_all.19 = f32[128,1,4352]{2,1,0:T(1,128)S(1)} all-to-all(f32[128,1,4352]{2,1,0:T(1,128)} %all_to_all.16), channel_id=1, replica_groups=mesh['layer'=128] {'layer'}, dimensions={0} | all-to-all | bytes 4456448 | tf_op jit(solution)/shard_map/all_to_all | solution.py:67
  307.6 0.7 copy.16
  308.3 3.3 all_to_all.14
  311.7 37.1 %all_to_all.20 = f32[128,1,4352]{2,1,0:T(1,128)S(1)} all-to-all(f32[128,1,4352]{2,1,0:T(1,128)} %all_to_all.14), channel_id=1, replica_groups=mesh['layer'=128] {'layer'}, dimensions={0} | all-to-all | bytes 4456448 | tf_op jit(solution)/shard_map/all_to_all | solution.py:72
  348.8 7.2 %reduce = f32[128,4352]{1,0:T(8,128)} reduce(f32[128,1,4352]{2,1,0:T(1,128)S(1)} %all_to_all.20, f32[]{:T(128)} %constant.9), dimensions={1}, to_apply=%all_to_all.15.reduce_sub_computation | reduce | bytes 4456452 | tf_op jit(solution)/shard_map/all_to_all | solution.py:72
  355.9 1.9 reshape.23
  357.9 1.6 fusion.7
  (17 shorter events, 2.4 us)
Async XLA Ops:
  0.6 26.9 %copy-start = (f32[1,512,512]{2,1,0:T(8,128)S(1)}, f32[1,512,512]{2,1,0:T(8,128)}, u32[]{:S(2)}) copy-start(f32[1,512,512]{2,1,0:T(8,128)} %param.4) | copy-start | bytes 3145732
  2.5 28.6 %copy-start.1 = (f32[1,512,512]{2,1,0:T(8,128)S(1)}, f32[1,512,512]{2,1,0:T(8,128)}, u32[]{:S(2)}) copy-start(f32[1,512,512]{2,1,0:T(8,128)} %param.3) | copy-start | bytes 3145732
  2.5 25.0 %collective-permute-start.1 = (f32[1088,512]{1,0:T(8,128)S(1)}, f32[1088,512]{1,0:T(8,128)S(1)}, u32[]{:S(2)}, u32[]{:S(2)}) collective-permute-start(f32[1088,512]{1,0:T(8,128)S(1)} %pad_maximum_fusion), channel_id=1, source_target_pairs={{0,127},{1,0},{2,1},{3,2},{4,3},{5,4},{6,5},{7,6},{8,7},{9,8},{10,... | collective-permute-start | bytes 6684680 | tf_op jit(solution)/shard_map/ppermute | solution.py:15
  2.6 28.4 %collective-permute-start = (f32[1088,512]{1,0:T(8,128)S(1)}, f32[1088,512]{1,0:T(8,128)S(1)}, u32[]{:S(2)}, u32[]{:S(2)}) collective-permute-start(f32[1088,512]{1,0:T(8,128)S(1)} %pad_maximum_fusion), channel_id=1, source_target_pairs={{0,1},{1,2},{2,3},{3,4},{4,5},{5,6},{6,7},{7,8},{8,9},{9,10},{10,1... | collective-permute-start | bytes 6684680 | tf_op jit(solution)/shard_map/ppermute | solution.py:15
  36.5 4.9 %copy-start.2 = (f32[1,64,512]{2,1,0:T(8,128)S(1)}, f32[1,64,512]{2,1,0:T(8,128)}, u32[]{:S(2)}) copy-start(f32[1,64,512]{2,1,0:T(8,128)} %param.5) | copy-start | bytes 393220
  64.4 50.5 %collective-permute-start.3 = (f32[1088,512]{1,0:T(8,128)S(1)}, f32[1088,512]{1,0:T(8,128)S(1)}, u32[]{:S(2)}, u32[]{:S(2)}) collective-permute-start(f32[1088,512]{1,0:T(8,128)S(1)} %pad_maximum_fusion.1), channel_id=1, source_target_pairs={{0,126},{1,127},{2,0},{3,1},{4,2},{5,3},{6,4},{7,5},{8,6},{9,7},{1... | collective-permute-start | bytes 6684680 | tf_op jit(solution)/shard_map/ppermute | solution.py:15
  76.5 50.4 %collective-permute-start.2 = (f32[1088,512]{1,0:T(8,128)S(1)}, f32[1088,512]{1,0:T(8,128)S(1)}, u32[]{:S(2)}, u32[]{:S(2)}) collective-permute-start(f32[1088,512]{1,0:T(8,128)S(1)} %pad_maximum_fusion.1), channel_id=1, source_target_pairs={{0,2},{1,3},{2,4},{3,5},{4,6},{5,7},{6,8},{7,9},{8,10},{9,11},{10,... | collective-permute-start | bytes 6684680 | tf_op jit(solution)/shard_map/ppermute | solution.py:15
  145.4 100.4 %collective-permute-start.5 = (f32[1088,512]{1,0:T(8,128)S(1)}, f32[1088,512]{1,0:T(8,128)S(1)}, u32[]{:S(2)}, u32[]{:S(2)}) collective-permute-start(f32[1088,512]{1,0:T(8,128)S(1)} %pad_maximum_fusion.2), channel_id=1, source_target_pairs={{0,124},{1,125},{2,126},{3,127},{4,0},{5,1},{6,2},{7,3},{8,4},{9,5... | collective-permute-start | bytes 6684680 | tf_op jit(solution)/shard_map/ppermute | solution.py:15
  149.5 98.2 %collective-permute-start.4 = (f32[1088,512]{1,0:T(8,128)S(1)}, f32[1088,512]{1,0:T(8,128)S(1)}, u32[]{:S(2)}, u32[]{:S(2)}) collective-permute-start(f32[1088,512]{1,0:T(8,128)S(1)} %pad_maximum_fusion.2), channel_id=1, source_target_pairs={{0,4},{1,5},{2,6},{3,7},{4,8},{5,9},{6,10},{7,11},{8,12},{9,13},{1... | collective-permute-start | bytes 6684680 | tf_op jit(solution)/shard_map/ppermute | solution.py:15
where the time goes:
time: 367 us; the launch traced here: 360 us
  waiting for transfers between devices  169 us (46%)
  matrix products  76.8 us (21%)
  blocking collectives  74.7 us (20%)
  starting transfers between devices  17.2 us (5%)
  other arithmetic  11.2 us (3%)
  local copies, waits for them, and re-layouts  10.5 us (3%)
    ppermute x6, waiting for transfers between devices, from_behind(): lax.ppermute(value, axis, [(i, (i + by) % peers) for i in range(peers)])  169 us
    dot_general x24, matrix products, matmul_high(): jnp.dot(left, right, precision=lax.Precision.HIGHEST, preferred_element_t...  66.4 us
    all_to_all x1, blocking collectives, per_device(): lax.all_to_all(flat_pieces, 'layer', split_axis=0, concat_axis=0, tiled=T...  37.6 us
    all_to_all x1, blocking collectives, per_device(): lax.all_to_all(spread_pieces, 'layer', split_axis=0, concat_axis=0, tiled...  37.1 us
    ppermute x6, starting transfers between devices, from_behind(): lax.ppermute(value, axis, [(i, (i + by) % peers) for i in range(peers)])  17.2 us
    dot_general x9, matrix products, rows_times(): lax.dot_general(columns, block, (((1,), (1,)), ((), ())), precision=lax.P...  10.4 us
  transfers between devices with their start and end apart: 6, of which 4 were waited for; matrix products, arithmetic and copies ran while one was open for 2% of the time, Pallas kernels for 0%

commit v1 on v0

v1 whole, which is shorter than its diff:
```python
import math

import jax
import jax.numpy as jnp
from jax import lax
from jax.sharding import PartitionSpec as P

BLOCK = 512
CHAINS = 8
LAYERS = 128
HIGH = lax.Precision.HIGH

LAST_LEVEL_BITS = ((6,), (0, 1, 5), (4,), (3,), (0, 1, 3, 4), (0, 3, 4, 5, 6), (1, 2, 3, 4, 5))


def last_level_device(layer):
    device = 0
    for bits in LAST_LEVEL_BITS:
        device = 2 * device + sum(layer >> bit for bit in bits) % 2
    return device ^ 2


def start_device(layer):
    return layer


def final_device(layer):
    return layer % CHAINS * (LAYERS // CHAINS) + layer // CHAINS


def move(value, source, target, partner=lambda layer: layer):
    pairs = [(source(i), target(partner(i) % LAYERS)) for i in range(LAYERS)]
    return lax.ppermute(value, "layer", pairs)


def stack(block, rhs):
    return jnp.concatenate([block, rhs], axis=0)


def matmul(left, right):
    return jnp.dot(left, right, precision=HIGH, preferred_element_type=jnp.float32)


def rows_times(block, columns):
    return lax.dot_general(
        columns,
        block,
        (((1,), (1,)), ((), ())),
        precision=HIGH,
        preferred_element_type=jnp.float32,
    )


def reduce_level(first, second, rhs, couple_first, couple_second, next_first, next_second):
    identity = jnp.eye(BLOCK, dtype=jnp.float32)
    coupling = matmul(first, couple_first) + matmul(second, couple_second)
    square = matmul(coupling, coupling)
    inverse = identity + coupling + square + matmul(coupling, square)
    inverse_first = matmul(inverse, first)
    inverse_second = matmul(inverse, second)
    new_second = -matmul(inverse_second, next_second[:BLOCK])
    new_first = -matmul(inverse_first, next_first[:BLOCK])
    new_rhs = (
        rows_times(inverse, rhs)
        - rows_times(inverse_first, next_first[BLOCK:])
        - rows_times(inverse_second, next_second[BLOCK:])
    )
    return new_first, new_second, new_rhs


def pair_level(first, second, rhs, place, bit):
    stride = 1 << bit

    def near(value):
        return move(value, place, place, lambda i: i ^ stride)

    def far(value):
        return move(value, place, place, lambda i: i + stride if i & stride else i - stride)

    couple_first = far(first)
    couple_second = near(second)
    next_first = far(stack(second, rhs))
    next_second = near(stack(first, rhs))
    return reduce_level(
        first, second, rhs, couple_first, couple_second, next_first, next_second
    )


def line_level(first, second, rhs, place, stride):
    def one(value):
        return move(value, place, place, lambda i: i - stride if i % 2 else i + stride)

    def two(value):
        return move(value, place, place, lambda i: i + stride if i % 2 else i - stride)

    couple_first = one(second)
    couple_second = two(first)
    next_first = one(stack(first, rhs))
    next_second = two(stack(second, rhs))
    return reduce_level(
        first, second, rhs, couple_first, couple_second, next_first, next_second
    )


def choose(condition, one, two):
    return jnp.where(condition, one, two), jnp.where(condition, two, one)


def per_device(lower_block, upper_block, right_side):
    layer = lax.axis_index("layer")
    rhs = right_side[0]
    first, second = choose(layer & 1 == 0, lower_block[0], upper_block[0])
    first, second, rhs = pair_level(first, second, rhs, start_device, 0)
    first, second, rhs = line_level(first, second, rhs, start_device, 2)
    first, second = choose((layer ^ (layer >> 2)) & 1 == 0, first, second)
    first = move(first, start_device, last_level_device)
    second_rhs = move(stack(second, rhs), start_device, last_level_device)
    second, rhs = second_rhs[:BLOCK], second_rhs[BLOCK:]
    first, second, rhs = pair_level(first, second, rhs, last_level_device, 2)
    first = move(first, last_level_device, final_device)
    second_rhs = move(stack(second, rhs), last_level_device, final_device)
    factor = 2.5**8 * math.sqrt(BLOCK)
    lower, upper = choose(layer & LAYERS // 2 == 0, first, second_rhs[:BLOCK])
    return (lower[None] * factor, upper[None] * factor, second_rhs[None, BLOCK:])


def solution(mesh):
    placed = (P("layer", None, None), P("layer", None, None), P("layer", None, None))
    return jax.shard_map(
        per_device,
        mesh=mesh,
        in_specs=placed,
        out_specs=placed,
        check_vma=False,
    )
```

time: 367 us -> 187 us (0.51); the launches traced: 360 us -> 187 us
  blocking collectives: 74.7 us -> 0 us
  waiting for transfers between devices: 169 us -> 118 us
  matrix products: 76.8 us -> 36 us
  local copies, waits for them, and re-layouts: 10.5 us -> 0.75 us
  starting transfers between devices: 17.2 us -> 25.1 us
  other arithmetic: 11.2 us -> 5.55 us
    all_to_all x2 -> x0, blocking collectives: 74.7 us -> none  [the longest x1 37.6 us: per_device(): lax.all_to_all(flat_pieces, 'layer', split_axis=0, concat_axis=0, tiled=T...]
    ppermute x6 -> x16, waiting for transfers between devices: 169 us -> 118 us  [move(): return lax.ppermute(value, 'layer', pairs)]
    dot_general x33, matrix products: 76.8 us -> 36 us  [the longest x24 29.5 us: matmul(): jnp.dot(left, right, precision=HIGH, preferred_element_type=jnp.float32)]
    ppermute x6 -> x16, starting transfers between devices: 17.2 us -> 25.1 us  [move(): return lax.ppermute(value, 'layer', pairs)]
    all_to_all x1 -> x0, other arithmetic: 7.17 us -> none  [per_device(): lax.all_to_all(spread_pieces, 'layer', split_axis=0, concat_axis=0, tiled...]
    all_to_all x2 -> x0, local copies, waits for them, and re-layouts: 7.02 us -> none  [the longest x1 3.7 us: per_device(): lax.all_to_all(flat_pieces, 'layer', split_axis=0, concat_axis=0, tiled=T...]
  transfers between devices with their start and end apart: 6 -> 16, of which waited for: 4 -> 11; matrix products, arithmetic and copies ran while one was open for 2% -> 19% of each run, Pallas kernels for 0% -> 0%
where the time goes in v1:
time: 187 us
  waiting for transfers between devices  118 us (63%)
  matrix products  36 us (19%)
  starting transfers between devices  25.1 us (13%)
  other arithmetic  5.55 us (3%)
    ppermute x16, waiting for transfers between devices, move(): return lax.ppermute(value, 'layer', pairs)  118 us
    dot_general x24, matrix products, matmul(): jnp.dot(left, right, precision=HIGH, preferred_element_type=jnp.float32)  29.5 us
    ppermute x16, starting transfers between devices, move(): return lax.ppermute(value, 'layer', pairs)  25.1 us
    dot_general x9, matrix products, rows_times(): lax.dot_general(columns, block, (((1,), (1,)), ((), ())), precision=HIGH,...  6.5 us
  transfers between devices with their start and end apart: 16, of which 11 were waited for; matrix products, arithmetic and copies ran while one was open for 19% of the time, Pallas kernels for 0%

profile of v1, /device:TPU:32, one launch (start us, length us, event | category | flops | bytes accessed | tf_op | source)
XLA Modules:
  0.0 186.9 jit_solution(9580651516026210240)
XLA Ops:
  0.6 1.8 select_bitcast_fusion.1
  2.7 1.7 pad_maximum_fusion.1
  4.4 1.7 collective-permute-start.2
  6.5 2.2 %fusion.26 = f32[512,512]{1,0:T(8,128)S(1)} fusion(f32[512,512]{1,0:T(8,128)S(1)} %get-tuple-element.8, f32[512,512]{1,0:T(8,128)} %collective-permute-done.1), kind=kOutput, calls=%fused_computation.61 | convolution fusion | flops 805306368 | bytes 3145728 | tf_op jit(solution)/shard_map/dot_general | solution.py:41
  8.7 8.3 %collective-permute-done = f32[512,512]{1,0:T(8,128)} collective-permute-done((f32[512,512]{1,0:T(8,128)S(1)}, f32[512,512]{1,0:T(8,128)}, u32[]{:S(2)}, u32[]{:S(2)}) %collective-permute-start) | collective-permute-done | bytes 1048608 | tf_op jit(solution)/shard_map/ppermute | solution.py:33
  17.0 2.3 %convolution_add_fusion.5 = f32[512,512]{1,0:T(8,128)S(1)} fusion(f32[512,512]{1,0:T(8,128)S(1)} %fusion.26, f32[512,512]{1,0:T(8,128)S(1)} %get-tuple-element.7, f32[512,512]{1,0:T(8,128)} %collective-permute-done), kind=kOutput, calls=%fused_computation.18 | convolution fusion | flops 805568512 | bytes 4194304 | tf_op jit(solution)/shard_map/dot_general | solution.py:41
  19.3 1.0 fusion.27
  20.3 1.0 convolution_add_fusion.4
  21.4 1.0 fusion.29
  22.4 1.0 fusion.28
  23.4 6.1 %collective-permute-done.2 = f32[576,512]{1,0:T(8,128)S(1)} collective-permute-done((f32[576,512]{1,0:T(8,128)}, f32[576,512]{1,0:T(8,128)S(1)}, u32[]{:S(2)}, u32[]{:S(2)}) %collective-permute-start.2) | collective-permute-done | bytes 1179680 | tf_op jit(solution)/shard_map/ppermute | solution.py:33
  29.5 1.0 convolution_negate_fusion.5
  30.6 7.1 %collective-permute-start.5 = (f32[512,512]{1,0:T(8,128)S(1)}, f32[512,512]{1,0:T(8,128)S(1)}, u32[]{:S(2)}, u32[]{:S(2)}) collective-permute-start(f32[512,512]{1,0:T(8,128)S(1)} %convolution_negate_fusion.5), channel_id=1, source_target_pairs={{0,126},{1,3},{2,0},{3,5},{4,2},{5,7},{6,4},{7,9},{8,6},{9,11},{10... | collective-permute-start | bytes 3145736 | tf_op jit(solution)/shard_map/ppermute | solution.py:33
  37.7 2.2 %convolution_negate_fusion.4 = f32[512,512]{1,0:T(8,128)S(1)} fusion(f32[512,512]{1,0:T(8,128)S(1)} %fusion.29, f32[576,512]{1,0:T(8,128)} %collective-permute-done.3), kind=kOutput, calls=%fused_computation.15 | convolution fusion | flops 805568512 | bytes 3145728 | tf_op jit(solution)/shard_map/dot_general | solution.py:41
  40.6 1.5 fusion.16
  43.0 2.1 %collective-permute-start.7 = (f32[576,512]{1,0:T(8,128)S(1)}, f32[576,512]{1,0:T(8,128)S(1)}, u32[]{:S(2)}, u32[]{:S(2)}) collective-permute-start(f32[576,512]{1,0:T(8,128)S(1)} %get-tuple-element.9), channel_id=1, source_target_pairs={{0,126},{1,3},{2,0},{3,5},{4,2},{5,7},{6,4},{7,9},{8,6},{9,11},{10... | collective-permute-start | bytes 3538952 | tf_op jit(solution)/shard_map/ppermute | solution.py:33
  45.1 16.2 %collective-permute-done.5 = f32[512,512]{1,0:T(8,128)S(1)} collective-permute-done((f32[512,512]{1,0:T(8,128)S(1)}, f32[512,512]{1,0:T(8,128)S(1)}, u32[]{:S(2)}, u32[]{:S(2)}) %collective-permute-start.5) | collective-permute-done | bytes 1048608 | tf_op jit(solution)/shard_map/ppermute | solution.py:33
  61.3 1.0 fusion.30
  62.4 1.3 collective-permute-done.4
  63.6 1.1 convolution_add_fusion.3
  64.7 1.0 fusion.31
  65.8 1.0 convolution_add_fusion.2
  66.8 0.6 fusion.34
  67.4 1.0 fusion.33
  68.5 1.0 fusion.32
  69.5 13.6 %collective-permute-done.7 = f32[576,512]{1,0:T(8,128)S(1)} collective-permute-done((f32[576,512]{1,0:T(8,128)S(1)}, f32[576,512]{1,0:T(8,128)S(1)}, u32[]{:S(2)}, u32[]{:S(2)}) %collective-permute-start.7) | collective-permute-done | bytes 1179680 | tf_op jit(solution)/shard_map/ppermute | solution.py:33
  83.1 1.0 convolution_negate_fusion.2
  85.5 1.1 broadcast_select_fusion.1
  86.6 5.1 %collective-permute-start.10 = (f32[576,512]{1,0:T(8,128)S(1)}, f32[576,512]{1,0:T(8,128)S(1)}, u32[]{:S(2)}, u32[]{:S(2)}) collective-permute-start(f32[576,512]{1,0:T(8,128)S(1)} %pad_maximum_fusion.4), channel_id=1, source_target_pairs={{0,2},{1,36},{2,39},{3,1},{4,3},{5,37},{6,38},{7,0},{8,13},{9,43},... | collective-permute-start | bytes 3538952 | tf_op jit(solution)/shard_map/ppermute | solution.py:33
  91.7 1.9 %collective-permute-start.8 = (f32[512,512]{1,0:T(8,128)S(1)}, f32[512,512]{1,0:T(8,128)S(1)}, u32[]{:S(2)}, u32[]{:S(2)}) collective-permute-start(f32[512,512]{1,0:T(8,128)S(1)} %get-tuple-element.5), channel_id=1, source_target_pairs={{0,2},{1,36},{2,39},{3,1},{4,3},{5,37},{6,38},{7,0},{8,13},{9,43},... | collective-permute-start | bytes 3145736 | tf_op jit(solution)/shard_map/ppermute | solution.py:33
  93.6 18.7 %collective-permute-done.10 = f32[576,512]{1,0:T(8,128)S(1)} collective-permute-done((f32[576,512]{1,0:T(8,128)S(1)}, f32[576,512]{1,0:T(8,128)S(1)}, u32[]{:S(2)}, u32[]{:S(2)}) %collective-permute-start.10) | collective-permute-done | bytes 1179680 | tf_op jit(solution)/shard_map/ppermute | solution.py:33
  112.5 11.1 %collective-permute-done.8 = f32[512,512]{1,0:T(8,128)S(1)} collective-permute-done((f32[512,512]{1,0:T(8,128)S(1)}, f32[512,512]{1,0:T(8,128)S(1)}, u32[]{:S(2)}, u32[]{:S(2)}) %collective-permute-start.8) | collective-permute-done | bytes 1048608 | tf_op jit(solution)/shard_map/ppermute | solution.py:33
  123.8 5.6 %collective-permute-start.12 = (f32[576,512]{1,0:T(8,128)S(1)}, f32[576,512]{1,0:T(8,128)S(1)}, u32[]{:S(2)}, u32[]{:S(2)}) collective-permute-start(f32[576,512]{1,0:T(8,128)S(1)} %collective-permute-done.10), channel_id=1, source_target_pairs={{2,122},{36,92},{39,95},{1,121},{3,13},{37,43},{38,40},{0,14},{13,... | collective-permute-start | bytes 3538952 | tf_op jit(solution)/shard_map/ppermute | solution.py:33
  129.4 1.0 fusion.24
  130.5 11.2 %collective-permute-done.9 = f32[512,512]{1,0:T(8,128)S(1)} collective-permute-done((f32[512,512]{1,0:T(8,128)S(1)}, f32[512,512]{1,0:T(8,128)S(1)}, u32[]{:S(2)}, u32[]{:S(2)}) %collective-permute-start.9) | collective-permute-done | bytes 1048608 | tf_op jit(solution)/shard_map/ppermute | solution.py:33
  141.7 1.0 convolution_add_fusion.1
  142.8 1.0 fusion.35
  143.8 1.0 convolution_add_fusion
  145.5 1.0 fusion.36
  146.6 1.0 fusion.22
  148.2 1.0 convolution_negate_fusion
  149.3 6.0 %collective-permute-done.12 = f32[576,512]{1,0:T(8,128)S(1)} collective-permute-done((f32[576,512]{1,0:T(8,128)S(1)}, f32[576,512]{1,0:T(8,128)S(1)}, u32[]{:S(2)}, u32[]{:S(2)}) %collective-permute-start.12) | collective-permute-done | bytes 1179680 | tf_op jit(solution)/shard_map/ppermute | solution.py:33
  156.0 0.6 collective-permute-start.15
  156.6 2.0 %convolution_negate_fusion.1 = f32[512,512]{1,0:T(8,128)} fusion(f32[512,512]{1,0:T(8,128)S(1)} %fusion.36, f32[576,512]{1,0:T(8,128)S(1)} %collective-permute-done.12), kind=kOutput, calls=%fused_computation.8 | convolution fusion | flops 805568512 | bytes 3145728 | tf_op jit(solution)/shard_map/dot_general | solution.py:41
  158.6 15.4 %collective-permute-done.15 = f32[576,512]{1,0:T(8,128)S(1)} collective-permute-done((f32[576,512]{1,0:T(8,128)S(1)}, f32[576,512]{1,0:T(8,128)S(1)}, u32[]{:S(2)}, u32[]{:S(2)}) %collective-permute-start.15) | collective-permute-done | bytes 1179680 | tf_op jit(solution)/shard_map/ppermute | solution.py:33
  174.1 0.7 slice_bitcast_fusion
  174.7 10.6 %collective-permute-done.13 = f32[512,512]{1,0:T(8,128)S(1)} collective-permute-done((f32[512,512]{1,0:T(8,128)}, f32[512,512]{1,0:T(8,128)S(1)}, u32[]{:S(2)}, u32[]{:S(2)}) %collective-permute-start.13) | collective-permute-done | bytes 1048608 | tf_op jit(solution)/shard_map/ppermute | solution.py:33
  185.3 1.6 multiply_bitcast_fusion
  (29 shorter events, 5.8 us)
Async XLA Ops:
  0.6 2.1 %copy-start = (f32[1,64,512]{2,1,0:T(8,128)S(1)}, f32[1,64,512]{2,1,0:T(8,128)}, u32[]{:S(2)}) copy-start(f32[1,64,512]{2,1,0:T(8,128)} %param.5) | copy-start | bytes 393220
  2.5 4.0 %collective-permute-start.1 = (f32[512,512]{1,0:T(8,128)S(1)}, f32[512,512]{1,0:T(8,128)}, u32[]{:S(2)}, u32[]{:S(2)}) collective-permute-start(f32[512,512]{1,0:T(8,128)S(1)} %get-tuple-element.8), channel_id=1, source_target_pairs={{0,1},{1,0},{2,3},{3,2},{4,5},{5,4},{6,7},{7,6},{8,9},{9,8},{10,11... | collective-permute-start | bytes 3145736 | tf_op jit(solution)/shard_map/ppermute | solution.py:33
  2.6 14.4 %collective-permute-start = (f32[512,512]{1,0:T(8,128)S(1)}, f32[512,512]{1,0:T(8,128)}, u32[]{:S(2)}, u32[]{:S(2)}) collective-permute-start(f32[512,512]{1,0:T(8,128)S(1)} %get-tuple-element.7), channel_id=1, source_target_pairs={{0,127},{1,2},{2,1},{3,4},{4,3},{5,6},{6,5},{7,8},{8,7},{9,10},{10... | collective-permute-start | bytes 3145736 | tf_op jit(solution)/shard_map/ppermute | solution.py:33
  4.4 25.2 %collective-permute-start.2 = (f32[576,512]{1,0:T(8,128)}, f32[576,512]{1,0:T(8,128)S(1)}, u32[]{:S(2)}, u32[]{:S(2)}) collective-permute-start(f32[576,512]{1,0:T(8,128)} %get-tuple-element.11), channel_id=1, source_target_pairs={{0,127},{1,2},{2,1},{3,4},{4,3},{5,6},{6,5},{7,8},{8,7},{9,10},{10... | collective-permute-start | bytes 3538952 | tf_op jit(solution)/shard_map/ppermute | solution.py:33
  6.1 31.6 %collective-permute-start.3 = (f32[576,512]{1,0:T(8,128)}, f32[576,512]{1,0:T(8,128)}, u32[]{:S(2)}, u32[]{:S(2)}) collective-permute-start(f32[576,512]{1,0:T(8,128)} %get-tuple-element.12), channel_id=1, source_target_pairs={{0,1},{1,0},{2,3},{3,2},{4,5},{5,4},{6,7},{7,6},{8,9},{9,8},{10,11... | collective-permute-start | bytes 3538952 | tf_op jit(solution)/shard_map/ppermute | solution.py:33
  30.6 30.8 %collective-permute-start.5 = (f32[512,512]{1,0:T(8,128)S(1)}, f32[512,512]{1,0:T(8,128)S(1)}, u32[]{:S(2)}, u32[]{:S(2)}) collective-permute-start(f32[512,512]{1,0:T(8,128)S(1)} %convolution_negate_fusion.5), channel_id=1, source_target_pairs={{0,126},{1,3},{2,0},{3,5},{4,2},{5,7},{6,4},{7,9},{8,6},{9,11},{10... | collective-permute-start | bytes 3145736 | tf_op jit(solution)/shard_map/ppermute | solution.py:33
  39.9 23.7 %collective-permute-start.4 = (f32[512,512]{1,0:T(8,128)S(1)}, f32[512,512]{1,0:T(8,128)S(1)}, u32[]{:S(2)}, u32[]{:S(2)}) collective-permute-start(f32[512,512]{1,0:T(8,128)S(1)} %convolution_negate_fusion.4), channel_id=1, source_target_pairs={{0,2},{1,127},{2,4},{3,1},{4,6},{5,3},{6,8},{7,5},{8,10},{9,7},{10... | collective-permute-start | bytes 3145736 | tf_op jit(solution)/shard_map/ppermute | solution.py:33
  43.0 40.1 %collective-permute-start.7 = (f32[576,512]{1,0:T(8,128)S(1)}, f32[576,512]{1,0:T(8,128)S(1)}, u32[]{:S(2)}, u32[]{:S(2)}) collective-permute-start(f32[576,512]{1,0:T(8,128)S(1)} %get-tuple-element.9), channel_id=1, source_target_pairs={{0,126},{1,3},{2,0},{3,5},{4,2},{5,7},{6,4},{7,9},{8,6},{9,11},{10... | collective-permute-start | bytes 3538952 | tf_op jit(solution)/shard_map/ppermute | solution.py:33
  45.1 39.1 %collective-permute-start.6 = (f32[576,512]{1,0:T(8,128)S(1)}, f32[576,512]{1,0:T(8,128)S(1)}, u32[]{:S(2)}, u32[]{:S(2)}) collective-permute-start(f32[576,512]{1,0:T(8,128)S(1)} %get-tuple-element.10), channel_id=1, source_target_pairs={{0,2},{1,127},{2,4},{3,1},{4,6},{5,3},{6,8},{7,5},{8,10},{9,7},{10... | collective-permute-start | bytes 3538952 | tf_op jit(solution)/shard_map/ppermute | solution.py:33
  86.6 25.8 %collective-permute-start.10 = (f32[576,512]{1,0:T(8,128)S(1)}, f32[576,512]{1,0:T(8,128)S(1)}, u32[]{:S(2)}, u32[]{:S(2)}) collective-permute-start(f32[576,512]{1,0:T(8,128)S(1)} %pad_maximum_fusion.4), channel_id=1, source_target_pairs={{0,2},{1,36},{2,39},{3,1},{4,3},{5,37},{6,38},{7,0},{8,13},{9,43},... | collective-permute-start | bytes 3538952 | tf_op jit(solution)/shard_map/ppermute | solution.py:33
  91.7 31.9 %collective-permute-start.8 = (f32[512,512]{1,0:T(8,128)S(1)}, f32[512,512]{1,0:T(8,128)S(1)}, u32[]{:S(2)}, u32[]{:S(2)}) collective-permute-start(f32[512,512]{1,0:T(8,128)S(1)} %get-tuple-element.5), channel_id=1, source_target_pairs={{0,2},{1,36},{2,39},{3,1},{4,3},{5,37},{6,38},{7,0},{8,13},{9,43},... | collective-permute-start | bytes 3145736 | tf_op jit(solution)/shard_map/ppermute | solution.py:33
  112.4 17.0 %collective-permute-start.11 = (f32[512,512]{1,0:T(8,128)S(1)}, f32[512,512]{1,0:T(8,128)S(1)}, u32[]{:S(2)}, u32[]{:S(2)}) collective-permute-start(f32[512,512]{1,0:T(8,128)S(1)} %slice.73), channel_id=1, source_target_pairs={{2,3},{36,37},{39,38},{1,0},{3,2},{37,36},{38,39},{0,1},{13,12},{4... | collective-permute-start | bytes 3145736 | tf_op jit(solution)/shard_map/ppermute | solution.py:33
  123.6 18.1 %collective-permute-start.9 = (f32[512,512]{1,0:T(8,128)S(1)}, f32[512,512]{1,0:T(8,128)S(1)}, u32[]{:S(2)}, u32[]{:S(2)}) collective-permute-start(f32[512,512]{1,0:T(8,128)S(1)} %collective-permute-done.8), channel_id=1, source_target_pairs={{2,122},{36,92},{39,95},{1,121},{3,13},{37,43},{38,40},{0,14},{13,... | collective-permute-start | bytes 3145736 | tf_op jit(solution)/shard_map/ppermute | solution.py:33
  123.7 23.9 %collective-permute-start.14 = (f32[576,512]{1,0:T(8,128)S(1)}, f32[576,512]{1,0:T(8,128)S(1)}, u32[]{:S(2)}, u32[]{:S(2)}) collective-permute-start(f32[576,512]{1,0:T(8,128)S(1)} %pad_maximum_fusion.5), channel_id=1, source_target_pairs={{2,3},{36,37},{39,38},{1,0},{3,2},{37,36},{38,39},{0,1},{13,12},{4... | collective-permute-start | bytes 3538952 | tf_op jit(solution)/shard_map/ppermute | solution.py:33
  123.8 31.4 %collective-permute-start.12 = (f32[576,512]{1,0:T(8,128)S(1)}, f32[576,512]{1,0:T(8,128)S(1)}, u32[]{:S(2)}, u32[]{:S(2)}) collective-permute-start(f32[576,512]{1,0:T(8,128)S(1)} %collective-permute-done.10), channel_id=1, source_target_pairs={{2,122},{36,92},{39,95},{1,121},{3,13},{37,43},{38,40},{0,14},{13,... | collective-permute-start | bytes 3538952 | tf_op jit(solution)/shard_map/ppermute | solution.py:33
  156.0 18.1 %collective-permute-start.15 = (f32[576,512]{1,0:T(8,128)S(1)}, f32[576,512]{1,0:T(8,128)S(1)}, u32[]{:S(2)}, u32[]{:S(2)}) collective-permute-start(f32[576,512]{1,0:T(8,128)S(1)} %pad_maximum_fusion.6), channel_id=1, source_target_pairs={{2,0},{36,16},{39,32},{1,48},{3,64},{37,80},{38,96},{0,112},{13,1}... | collective-permute-start | bytes 3538952 | tf_op jit(solution)/shard_map/ppermute | solution.py:33
  158.6 26.7 %collective-permute-start.13 = (f32[512,512]{1,0:T(8,128)}, f32[512,512]{1,0:T(8,128)S(1)}, u32[]{:S(2)}, u32[]{:S(2)}) collective-permute-start(f32[512,512]{1,0:T(8,128)} %convolution_negate_fusion.1), channel_id=1, source_target_pairs={{2,0},{36,16},{39,32},{1,48},{3,64},{37,80},{38,96},{0,112},{13,1}... | collective-permute-start | bytes 3145736 | tf_op jit(solution)/shard_map/ppermute | solution.py:33

commit v2 on v1

--- a/solution.py
+++ b/solution.py
@@ -8,7 +8,7 @@
 BLOCK = 512
 CHAINS = 8
 LAYERS = 128
-HIGH = lax.Precision.HIGH
+HIGH, HIGHEST = lax.Precision.HIGH, lax.Precision.HIGHEST
 
 LAST_LEVEL_BITS = ((6,), (0, 1, 5), (4,), (3,), (0, 1, 3, 4), (0, 3, 4, 5, 6), (1, 2, 3, 4, 5))
 
@@ -37,8 +37,8 @@
     return jnp.concatenate([block, rhs], axis=0)
 
 
-def matmul(left, right):
-    return jnp.dot(left, right, precision=HIGH, preferred_element_type=jnp.float32)
+def matmul(left, right, precision=HIGH):
+    return jnp.dot(left, right, precision=precision, preferred_element_type=jnp.float32)
 
 
 def rows_times(block, columns):
@@ -51,13 +51,15 @@
     )
 
 
-def reduce_level(first, second, rhs, couple_first, couple_second, next_first, next_second):
+def reduce_level(
+    first, second, rhs, couple_first, couple_second, next_first, next_second, precision
+):
     identity = jnp.eye(BLOCK, dtype=jnp.float32)
     coupling = matmul(first, couple_first) + matmul(second, couple_second)
     square = matmul(coupling, coupling)
     inverse = identity + coupling + square + matmul(coupling, square)
-    inverse_first = matmul(inverse, first)
-    inverse_second = matmul(inverse, second)
+    inverse_first = matmul(inverse, first, precision)
+    inverse_second = matmul(inverse, second, precision)
     new_second = -matmul(inverse_second, next_second[:BLOCK])
     new_first = -matmul(inverse_first, next_first[:BLOCK])
     new_rhs = (
@@ -68,7 +70,7 @@
     return new_first, new_second, new_rhs
 
 
-def pair_level(first, second, rhs, place, bit):
+def pair_level(first, second, rhs, place, bit, precision):
     stride = 1 << bit
 
     def near(value):
@@ -82,7 +84,7 @@
     next_first = far(stack(second, rhs))
     next_second = near(stack(first, rhs))
     return reduce_level(
-        first, second, rhs, couple_first, couple_second, next_first, next_second
+        first, second, rhs, couple_first, couple_second, next_first, next_second, precision
     )
 
 
@@ -98,7 +100,7 @@
     next_first = one(stack(first, rhs))
     next_second = two(stack(second, rhs))
     return reduce_level(
-        first, second, rhs, couple_first, couple_second, next_first, next_second
+        first, second, rhs, couple_first, couple_second, next_first, next_second, HIGHEST
     )
 
 
@@ -110,13 +112,13 @@
     layer = lax.axis_index("layer")
     rhs = right_side[0]
     first, second = choose(layer & 1 == 0, lower_block[0], upper_block[0])
-    first, second, rhs = pair_level(first, second, rhs, start_device, 0)
+    first, second, rhs = pair_level(first, second, rhs, start_device, 0, HIGHEST)
     first, second, rhs = line_level(first, second, rhs, start_device, 2)
     first, second = choose((layer ^ (layer >> 2)) & 1 == 0, first, second)
     first = move(first, start_device, last_level_device)
     second_rhs = move(stack(second, rhs), start_device, last_level_device)
     second, rhs = second_rhs[:BLOCK], second_rhs[BLOCK:]
-    first, second, rhs = pair_level(first, second, rhs, last_level_device, 2)
+    first, second, rhs = pair_level(first, second, rhs, last_level_device, 2, HIGH)
     first = move(first, last_level_device, final_device)
     second_rhs = move(stack(second, rhs), last_level_device, final_device)
     factor = 2.5**8 * math.sqrt(BLOCK)

time: 187 us -> 187 us (level)
  matrix products: 36 us -> 39.3 us
  waiting for transfers between devices: 118 us -> 115 us
    dot_general x24, matrix products: 29.5 us -> 32.8 us  [matmul(): jnp.dot(left, right, precision=precision, preferred_element_type=jnp.floa...]
    ppermute x16, waiting for transfers between devices: 118 us -> 115 us  [move(): return lax.ppermute(value, 'layer', pairs)]
  transfers between devices with their start and end apart: 16 -> 16, of which waited for: 11 -> 11; matrix products, arithmetic and copies ran while one was open for 19% -> 21% of each run, Pallas kernels for 0% -> 0%
where the time goes in v2:
time: 187 us
  waiting for transfers between devices  115 us (61%)
  matrix products  39.3 us (21%)
  starting transfers between devices  25.1 us (13%)
  other arithmetic  5.55 us (3%)
    ppermute x16, waiting for transfers between devices, move(): return lax.ppermute(value, 'layer', pairs)  115 us
    dot_general x24, matrix products, matmul(): jnp.dot(left, right, precision=precision, preferred_element_type=jnp.floa...  32.8 us
    ppermute x16, starting transfers between devices, move(): return lax.ppermute(value, 'layer', pairs)  25.1 us
    dot_general x9, matrix products, rows_times(): lax.dot_general(columns, block, (((1,), (1,)), ((), ())), precision=HIGH,...  6.5 us
  transfers between devices with their start and end apart: 16, of which 11 were waited for; matrix products, arithmetic and copies ran while one was open for 21% of the time, Pallas kernels for 0%

profile of v2, /device:TPU:32, one launch (start us, length us, event | category | flops | bytes accessed | tf_op | source)
XLA Modules:
  0.0 186.9 jit_solution(5288294495884059145)
XLA Ops:
  0.6 1.8 select_bitcast_fusion.1
  2.7 1.7 pad_maximum_fusion.1
  4.4 1.7 collective-permute-start.2
  6.5 2.2 %fusion.26 = f32[512,512]{1,0:T(8,128)S(1)} fusion(f32[512,512]{1,0:T(8,128)S(1)} %get-tuple-element.8, f32[512,512]{1,0:T(8,128)} %collective-permute-done.1), kind=kOutput, calls=%fused_computation.61 | convolution fusion | flops 805306368 | bytes 3145728 | tf_op jit(solution)/shard_map/dot_general | solution.py:41
  8.7 8.3 %collective-permute-done = f32[512,512]{1,0:T(8,128)} collective-permute-done((f32[512,512]{1,0:T(8,128)S(1)}, f32[512,512]{1,0:T(8,128)}, u32[]{:S(2)}, u32[]{:S(2)}) %collective-permute-start) | collective-permute-done | bytes 1048608 | tf_op jit(solution)/shard_map/ppermute | solution.py:33
  17.0 2.3 %convolution_add_fusion.5 = f32[512,512]{1,0:T(8,128)S(1)} fusion(f32[512,512]{1,0:T(8,128)S(1)} %fusion.26, f32[512,512]{1,0:T(8,128)S(1)} %get-tuple-element.7, f32[512,512]{1,0:T(8,128)} %collective-permute-done), kind=kOutput, calls=%fused_computation.18 | convolution fusion | flops 805568512 | bytes 4194304 | tf_op jit(solution)/shard_map/dot_general | solution.py:41
  19.3 1.0 fusion.27
  20.3 1.0 convolution_add_fusion.4
  21.4 1.9 fusion.29
  23.2 1.9 fusion.28
  25.1 4.4 %collective-permute-done.2 = f32[576,512]{1,0:T(8,128)S(1)} collective-permute-done((f32[576,512]{1,0:T(8,128)}, f32[576,512]{1,0:T(8,128)S(1)}, u32[]{:S(2)}, u32[]{:S(2)}) %collective-permute-start.2) | collective-permute-done | bytes 1179680 | tf_op jit(solution)/shard_map/ppermute | solution.py:33
  29.5 1.0 convolution_negate_fusion.5
  30.6 7.1 %collective-permute-start.5 = (f32[512,512]{1,0:T(8,128)S(1)}, f32[512,512]{1,0:T(8,128)S(1)}, u32[]{:S(2)}, u32[]{:S(2)}) collective-permute-start(f32[512,512]{1,0:T(8,128)S(1)} %convolution_negate_fusion.5), channel_id=1, source_target_pairs={{0,126},{1,3},{2,0},{3,5},{4,2},{5,7},{6,4},{7,9},{8,6},{9,11},{10... | collective-permute-start | bytes 3145736 | tf_op jit(solution)/shard_map/ppermute | solution.py:33
  37.7 2.2 %convolution_negate_fusion.4 = f32[512,512]{1,0:T(8,128)S(1)} fusion(f32[512,512]{1,0:T(8,128)S(1)} %fusion.29, f32[576,512]{1,0:T(8,128)} %collective-permute-done.3), kind=kOutput, calls=%fused_computation.15 | convolution fusion | flops 805568512 | bytes 3145728 | tf_op jit(solution)/shard_map/dot_general | solution.py:41
  40.6 1.5 fusion.16
  43.0 2.1 %collective-permute-start.7 = (f32[576,512]{1,0:T(8,128)S(1)}, f32[576,512]{1,0:T(8,128)S(1)}, u32[]{:S(2)}, u32[]{:S(2)}) collective-permute-start(f32[576,512]{1,0:T(8,128)S(1)} %get-tuple-element.9), channel_id=1, source_target_pairs={{0,126},{1,3},{2,0},{3,5},{4,2},{5,7},{6,4},{7,9},{8,6},{9,11},{10... | collective-permute-start | bytes 3538952 | tf_op jit(solution)/shard_map/ppermute | solution.py:33
  45.1 16.2 %collective-permute-done.5 = f32[512,512]{1,0:T(8,128)S(1)} collective-permute-done((f32[512,512]{1,0:T(8,128)S(1)}, f32[512,512]{1,0:T(8,128)S(1)}, u32[]{:S(2)}, u32[]{:S(2)}) %collective-permute-start.5) | collective-permute-done | bytes 1048608 | tf_op jit(solution)/shard_map/ppermute | solution.py:33
  61.3 1.0 fusion.30
  62.4 1.3 collective-permute-done.4
  63.6 1.1 convolution_add_fusion.3
  64.7 1.0 fusion.31
  65.8 1.0 convolution_add_fusion.2
  66.8 0.6 fusion.34
  67.4 1.9 fusion.33
  69.3 1.9 fusion.32
  71.2 12.0 %collective-permute-done.7 = f32[576,512]{1,0:T(8,128)S(1)} collective-permute-done((f32[576,512]{1,0:T(8,128)S(1)}, f32[576,512]{1,0:T(8,128)S(1)}, u32[]{:S(2)}, u32[]{:S(2)}) %collective-permute-start.7) | collective-permute-done | bytes 1179680 | tf_op jit(solution)/shard_map/ppermute | solution.py:33
  83.1 1.0 convolution_negate_fusion.2
  85.5 1.1 broadcast_select_fusion.1
  86.6 5.1 %collective-permute-start.10 = (f32[576,512]{1,0:T(8,128)S(1)}, f32[576,512]{1,0:T(8,128)S(1)}, u32[]{:S(2)}, u32[]{:S(2)}) collective-permute-start(f32[576,512]{1,0:T(8,128)S(1)} %pad_maximum_fusion.4), channel_id=1, source_target_pairs={{0,2},{1,36},{2,39},{3,1},{4,3},{5,37},{6,38},{7,0},{8,13},{9,43},... | collective-permute-start | bytes 3538952 | tf_op jit(solution)/shard_map/ppermute | solution.py:33
  91.7 1.9 %collective-permute-start.8 = (f32[512,512]{1,0:T(8,128)S(1)}, f32[512,512]{1,0:T(8,128)S(1)}, u32[]{:S(2)}, u32[]{:S(2)}) collective-permute-start(f32[512,512]{1,0:T(8,128)S(1)} %get-tuple-element.5), channel_id=1, source_target_pairs={{0,2},{1,36},{2,39},{3,1},{4,3},{5,37},{6,38},{7,0},{8,13},{9,43},... | collective-permute-start | bytes 3145736 | tf_op jit(solution)/shard_map/ppermute | solution.py:33
  93.6 18.7 %collective-permute-done.10 = f32[576,512]{1,0:T(8,128)S(1)} collective-permute-done((f32[576,512]{1,0:T(8,128)S(1)}, f32[576,512]{1,0:T(8,128)S(1)}, u32[]{:S(2)}, u32[]{:S(2)}) %collective-permute-start.10) | collective-permute-done | bytes 1179680 | tf_op jit(solution)/shard_map/ppermute | solution.py:33
  112.5 11.1 %collective-permute-done.8 = f32[512,512]{1,0:T(8,128)S(1)} collective-permute-done((f32[512,512]{1,0:T(8,128)S(1)}, f32[512,512]{1,0:T(8,128)S(1)}, u32[]{:S(2)}, u32[]{:S(2)}) %collective-permute-start.8) | collective-permute-done | bytes 1048608 | tf_op jit(solution)/shard_map/ppermute | solution.py:33
  123.8 5.6 %collective-permute-start.12 = (f32[576,512]{1,0:T(8,128)S(1)}, f32[576,512]{1,0:T(8,128)S(1)}, u32[]{:S(2)}, u32[]{:S(2)}) collective-permute-start(f32[576,512]{1,0:T(8,128)S(1)} %collective-permute-done.10), channel_id=1, source_target_pairs={{2,122},{36,92},{39,95},{1,121},{3,13},{37,43},{38,40},{0,14},{13,... | collective-permute-start | bytes 3538952 | tf_op jit(solution)/shard_map/ppermute | solution.py:33
  129.4 1.0 fusion.24
  130.5 11.2 %collective-permute-done.9 = f32[512,512]{1,0:T(8,128)S(1)} collective-permute-done((f32[512,512]{1,0:T(8,128)S(1)}, f32[512,512]{1,0:T(8,128)S(1)}, u32[]{:S(2)}, u32[]{:S(2)}) %collective-permute-start.9) | collective-permute-done | bytes 1048608 | tf_op jit(solution)/shard_map/ppermute | solution.py:33
  141.7 1.0 convolution_add_fusion.1
  142.8 1.0 fusion.35
  143.8 1.0 convolution_add_fusion
  145.5 1.0 fusion.36
  146.6 1.0 fusion.22
  148.2 1.0 convolution_negate_fusion
  149.3 6.0 %collective-permute-done.12 = f32[576,512]{1,0:T(8,128)S(1)} collective-permute-done((f32[576,512]{1,0:T(8,128)S(1)}, f32[576,512]{1,0:T(8,128)S(1)}, u32[]{:S(2)}, u32[]{:S(2)}) %collective-permute-start.12) | collective-permute-done | bytes 1179680 | tf_op jit(solution)/shard_map/ppermute | solution.py:33
  156.0 0.6 collective-permute-start.15
  156.6 2.0 %convolution_negate_fusion.1 = f32[512,512]{1,0:T(8,128)} fusion(f32[512,512]{1,0:T(8,128)S(1)} %fusion.36, f32[576,512]{1,0:T(8,128)S(1)} %collective-permute-done.12), kind=kOutput, calls=%fused_computation.8 | convolution fusion | flops 805568512 | bytes 3145728 | tf_op jit(solution)/shard_map/dot_general | solution.py:41
  158.6 15.4 %collective-permute-done.15 = f32[576,512]{1,0:T(8,128)S(1)} collective-permute-done((f32[576,512]{1,0:T(8,128)S(1)}, f32[576,512]{1,0:T(8,128)S(1)}, u32[]{:S(2)}, u32[]{:S(2)}) %collective-permute-start.15) | collective-permute-done | bytes 1179680 | tf_op jit(solution)/shard_map/ppermute | solution.py:33
  174.1 0.7 slice_bitcast_fusion
  174.7 10.6 %collective-permute-done.13 = f32[512,512]{1,0:T(8,128)S(1)} collective-permute-done((f32[512,512]{1,0:T(8,128)}, f32[512,512]{1,0:T(8,128)S(1)}, u32[]{:S(2)}, u32[]{:S(2)}) %collective-permute-start.13) | collective-permute-done | bytes 1048608 | tf_op jit(solution)/shard_map/ppermute | solution.py:33
  185.3 1.6 multiply_bitcast_fusion
  (29 shorter events, 5.8 us)
Async XLA Ops:
  0.6 2.1 %copy-start = (f32[1,64,512]{2,1,0:T(8,128)S(1)}, f32[1,64,512]{2,1,0:T(8,128)}, u32[]{:S(2)}) copy-start(f32[1,64,512]{2,1,0:T(8,128)} %param.5) | copy-start | bytes 393220
  2.5 4.0 %collective-permute-start.1 = (f32[512,512]{1,0:T(8,128)S(1)}, f32[512,512]{1,0:T(8,128)}, u32[]{:S(2)}, u32[]{:S(2)}) collective-permute-start(f32[512,512]{1,0:T(8,128)S(1)} %get-tuple-element.8), channel_id=1, source_target_pairs={{0,1},{1,0},{2,3},{3,2},{4,5},{5,4},{6,7},{7,6},{8,9},{9,8},{10,11... | collective-permute-start | bytes 3145736 | tf_op jit(solution)/shard_map/ppermute | solution.py:33
  2.6 14.4 %collective-permute-start = (f32[512,512]{1,0:T(8,128)S(1)}, f32[512,512]{1,0:T(8,128)}, u32[]{:S(2)}, u32[]{:S(2)}) collective-permute-start(f32[512,512]{1,0:T(8,128)S(1)} %get-tuple-element.7), channel_id=1, source_target_pairs={{0,127},{1,2},{2,1},{3,4},{4,3},{5,6},{6,5},{7,8},{8,7},{9,10},{10... | collective-permute-start | bytes 3145736 | tf_op jit(solution)/shard_map/ppermute | solution.py:33
  4.4 25.2 %collective-permute-start.2 = (f32[576,512]{1,0:T(8,128)}, f32[576,512]{1,0:T(8,128)S(1)}, u32[]{:S(2)}, u32[]{:S(2)}) collective-permute-start(f32[576,512]{1,0:T(8,128)} %get-tuple-element.11), channel_id=1, source_target_pairs={{0,127},{1,2},{2,1},{3,4},{4,3},{5,6},{6,5},{7,8},{8,7},{9,10},{10... | collective-permute-start | bytes 3538952 | tf_op jit(solution)/shard_map/ppermute | solution.py:33
  6.1 31.6 %collective-permute-start.3 = (f32[576,512]{1,0:T(8,128)}, f32[576,512]{1,0:T(8,128)}, u32[]{:S(2)}, u32[]{:S(2)}) collective-permute-start(f32[576,512]{1,0:T(8,128)} %get-tuple-element.12), channel_id=1, source_target_pairs={{0,1},{1,0},{2,3},{3,2},{4,5},{5,4},{6,7},{7,6},{8,9},{9,8},{10,11... | collective-permute-start | bytes 3538952 | tf_op jit(solution)/shard_map/ppermute | solution.py:33
  30.6 30.8 %collective-permute-start.5 = (f32[512,512]{1,0:T(8,128)S(1)}, f32[512,512]{1,0:T(8,128)S(1)}, u32[]{:S(2)}, u32[]{:S(2)}) collective-permute-start(f32[512,512]{1,0:T(8,128)S(1)} %convolution_negate_fusion.5), channel_id=1, source_target_pairs={{0,126},{1,3},{2,0},{3,5},{4,2},{5,7},{6,4},{7,9},{8,6},{9,11},{10... | collective-permute-start | bytes 3145736 | tf_op jit(solution)/shard_map/ppermute | solution.py:33
  39.9 23.7 %collective-permute-start.4 = (f32[512,512]{1,0:T(8,128)S(1)}, f32[512,512]{1,0:T(8,128)S(1)}, u32[]{:S(2)}, u32[]{:S(2)}) collective-permute-start(f32[512,512]{1,0:T(8,128)S(1)} %convolution_negate_fusion.4), channel_id=1, source_target_pairs={{0,2},{1,127},{2,4},{3,1},{4,6},{5,3},{6,8},{7,5},{8,10},{9,7},{10... | collective-permute-start | bytes 3145736 | tf_op jit(solution)/shard_map/ppermute | solution.py:33
  43.0 40.1 %collective-permute-start.7 = (f32[576,512]{1,0:T(8,128)S(1)}, f32[576,512]{1,0:T(8,128)S(1)}, u32[]{:S(2)}, u32[]{:S(2)}) collective-permute-start(f32[576,512]{1,0:T(8,128)S(1)} %get-tuple-element.9), channel_id=1, source_target_pairs={{0,126},{1,3},{2,0},{3,5},{4,2},{5,7},{6,4},{7,9},{8,6},{9,11},{10... | collective-permute-start | bytes 3538952 | tf_op jit(solution)/shard_map/ppermute | solution.py:33
  45.1 39.1 %collective-permute-start.6 = (f32[576,512]{1,0:T(8,128)S(1)}, f32[576,512]{1,0:T(8,128)S(1)}, u32[]{:S(2)}, u32[]{:S(2)}) collective-permute-start(f32[576,512]{1,0:T(8,128)S(1)} %get-tuple-element.10), channel_id=1, source_target_pairs={{0,2},{1,127},{2,4},{3,1},{4,6},{5,3},{6,8},{7,5},{8,10},{9,7},{10... | collective-permute-start | bytes 3538952 | tf_op jit(solution)/shard_map/ppermute | solution.py:33
  86.6 25.8 %collective-permute-start.10 = (f32[576,512]{1,0:T(8,128)S(1)}, f32[576,512]{1,0:T(8,128)S(1)}, u32[]{:S(2)}, u32[]{:S(2)}) collective-permute-start(f32[576,512]{1,0:T(8,128)S(1)} %pad_maximum_fusion.4), channel_id=1, source_target_pairs={{0,2},{1,36},{2,39},{3,1},{4,3},{5,37},{6,38},{7,0},{8,13},{9,43},... | collective-permute-start | bytes 3538952 | tf_op jit(solution)/shard_map/ppermute | solution.py:33
  91.7 31.9 %collective-permute-start.8 = (f32[512,512]{1,0:T(8,128)S(1)}, f32[512,512]{1,0:T(8,128)S(1)}, u32[]{:S(2)}, u32[]{:S(2)}) collective-permute-start(f32[512,512]{1,0:T(8,128)S(1)} %get-tuple-element.5), channel_id=1, source_target_pairs={{0,2},{1,36},{2,39},{3,1},{4,3},{5,37},{6,38},{7,0},{8,13},{9,43},... | collective-permute-start | bytes 3145736 | tf_op jit(solution)/shard_map/ppermute | solution.py:33
  112.4 17.0 %collective-permute-start.11 = (f32[512,512]{1,0:T(8,128)S(1)}, f32[512,512]{1,0:T(8,128)S(1)}, u32[]{:S(2)}, u32[]{:S(2)}) collective-permute-start(f32[512,512]{1,0:T(8,128)S(1)} %slice.73), channel_id=1, source_target_pairs={{2,3},{36,37},{39,38},{1,0},{3,2},{37,36},{38,39},{0,1},{13,12},{4... | collective-permute-start | bytes 3145736 | tf_op jit(solution)/shard_map/ppermute | solution.py:33
  123.6 18.1 %collective-permute-start.9 = (f32[512,512]{1,0:T(8,128)S(1)}, f32[512,512]{1,0:T(8,128)S(1)}, u32[]{:S(2)}, u32[]{:S(2)}) collective-permute-start(f32[512,512]{1,0:T(8,128)S(1)} %collective-permute-done.8), channel_id=1, source_target_pairs={{2,122},{36,92},{39,95},{1,121},{3,13},{37,43},{38,40},{0,14},{13,... | collective-permute-start | bytes 3145736 | tf_op jit(solution)/shard_map/ppermute | solution.py:33
  123.7 23.9 %collective-permute-start.14 = (f32[576,512]{1,0:T(8,128)S(1)}, f32[576,512]{1,0:T(8,128)S(1)}, u32[]{:S(2)}, u32[]{:S(2)}) collective-permute-start(f32[576,512]{1,0:T(8,128)S(1)} %pad_maximum_fusion.5), channel_id=1, source_target_pairs={{2,3},{36,37},{39,38},{1,0},{3,2},{37,36},{38,39},{0,1},{13,12},{4... | collective-permute-start | bytes 3538952 | tf_op jit(solution)/shard_map/ppermute | solution.py:33
  123.8 31.4 %collective-permute-start.12 = (f32[576,512]{1,0:T(8,128)S(1)}, f32[576,512]{1,0:T(8,128)S(1)}, u32[]{:S(2)}, u32[]{:S(2)}) collective-permute-start(f32[576,512]{1,0:T(8,128)S(1)} %collective-permute-done.10), channel_id=1, source_target_pairs={{2,122},{36,92},{39,95},{1,121},{3,13},{37,43},{38,40},{0,14},{13,... | collective-permute-start | bytes 3538952 | tf_op jit(solution)/shard_map/ppermute | solution.py:33
  156.0 18.1 %collective-permute-start.15 = (f32[576,512]{1,0:T(8,128)S(1)}, f32[576,512]{1,0:T(8,128)S(1)}, u32[]{:S(2)}, u32[]{:S(2)}) collective-permute-start(f32[576,512]{1,0:T(8,128)S(1)} %pad_maximum_fusion.6), channel_id=1, source_target_pairs={{2,0},{36,16},{39,32},{1,48},{3,64},{37,80},{38,96},{0,112},{13,1}... | collective-permute-start | bytes 3538952 | tf_op jit(solution)/shard_map/ppermute | solution.py:33
  158.6 26.7 %collective-permute-start.13 = (f32[512,512]{1,0:T(8,128)}, f32[512,512]{1,0:T(8,128)S(1)}, u32[]{:S(2)}, u32[]{:S(2)}) collective-permute-start(f32[512,512]{1,0:T(8,128)} %convolution_negate_fusion.1), channel_id=1, source_target_pairs={{2,0},{36,16},{39,32},{1,48},{3,64},{37,80},{38,96},{0,112},{13,1}... | collective-permute-start | bytes 3145736 | tf_op jit(solution)/shard_map/ppermute | solution.py:33

commit v3 on v2

--- a/solution.py
+++ b/solution.py
@@ -88,6 +88,31 @@
     )
 
 
+def last_level(first_rhs, second):
+    place = last_level_device
+
+    def near(value):
+        return move(value, place, place, lambda i: i ^ 4)
+
+    def far(value):
+        return move(value, place, place, lambda i: i + 4 if i & 4 else i - 4)
+
+    couple_first = far(first_rhs)
+    couple_second = near(second)
+    next_first = stack(far(second), couple_first[BLOCK:])
+    next_second = near(first_rhs)
+    return reduce_level(
+        first_rhs[:BLOCK],
+        second,
+        first_rhs[BLOCK:],
+        couple_first[:BLOCK],
+        couple_second,
+        next_first,
+        next_second,
+        HIGH,
+    )
+
+
 def line_level(first, second, rhs, place, stride):
     def one(value):
         return move(value, place, place, lambda i: i - stride if i % 2 else i + stride)
@@ -115,15 +140,15 @@
     first, second, rhs = pair_level(first, second, rhs, start_device, 0, HIGHEST)
     first, second, rhs = line_level(first, second, rhs, start_device, 2)
     first, second = choose((layer ^ (layer >> 2)) & 1 == 0, first, second)
-    first = move(first, start_device, last_level_device)
-    second_rhs = move(stack(second, rhs), start_device, last_level_device)
-    second, rhs = second_rhs[:BLOCK], second_rhs[BLOCK:]
-    first, second, rhs = pair_level(first, second, rhs, last_level_device, 2, HIGH)
+    first_rhs = move(stack(first, rhs), start_device, last_level_device)
+    second = move(second, start_device, last_level_device)
+    first, second, rhs = last_level(first_rhs, second)
+    second = move(second, last_level_device, final_device)
     first = move(first, last_level_device, final_device)
-    second_rhs = move(stack(second, rhs), last_level_device, final_device)
+    rhs = move(rhs, last_level_device, final_device)
     factor = 2.5**8 * math.sqrt(BLOCK)
-    lower, upper = choose(layer & LAYERS // 2 == 0, first, second_rhs[:BLOCK])
-    return (lower[None] * factor, upper[None] * factor, second_rhs[None, BLOCK:])
+    lower, upper = choose(layer & LAYERS // 2 == 0, first, second)
+    return (lower[None] * factor, upper[None] * factor, rhs[None])
 
 
 def solution(mesh):

time: 187 us -> 210 us (1.12)
  the two profiles are of different devices: /device:TPU:32 before, /device:TPU:16 now
where the time goes in v3:
time: 210 us; the launch traced here: 209 us
  waiting for transfers between devices  134 us (64%)
  matrix products  39.4 us (19%)
  starting transfers between devices  28.6 us (14%)
  other arithmetic  5.39 us (3%)
    ppermute x17, waiting for transfers between devices, move(): return lax.ppermute(value, 'layer', pairs)  134 us
    dot_general x24, matrix products, matmul(): jnp.dot(left, right, precision=precision, preferred_element_type=jnp.floa...  32.9 us
    ppermute x17, starting transfers between devices, move(): return lax.ppermute(value, 'layer', pairs)  28.6 us
    dot_general x9, matrix products, rows_times(): lax.dot_general(columns, block, (((1,), (1,)), ((), ())), precision=HIGH,...  6.52 us
  transfers between devices with their start and end apart: 17, of which 11 were waited for; matrix products, arithmetic and copies ran while one was open for 19% of the time, Pallas kernels for 0%

profile of v3, /device:TPU:16, one launch (start us, length us, event | category | flops | bytes accessed | tf_op | source)
XLA Modules:
  0.0 209.3 jit_solution(14941818090698733816)
XLA Ops:
  0.6 1.8 select_bitcast_fusion.1
  2.6 4.0 %collective-permute-start = (f32[512,512]{1,0:T(8,128)S(1)}, f32[512,512]{1,0:T(8,128)}, u32[]{:S(2)}, u32[]{:S(2)}) collective-permute-start(f32[512,512]{1,0:T(8,128)S(1)} %get-tuple-element.7), channel_id=1, source_target_pairs={{0,127},{1,2},{2,1},{3,4},{4,3},{5,6},{6,5},{7,8},{8,7},{9,10},{10... | collective-permute-start | bytes 3145736 | tf_op jit(solution)/shard_map/ppermute | solution.py:33
  6.6 1.7 pad_maximum_fusion.1
  8.8 2.2 %fusion.23 = f32[512,512]{1,0:T(8,128)S(1)} fusion(f32[512,512]{1,0:T(8,128)S(1)} %get-tuple-element.8, f32[512,512]{1,0:T(8,128)} %collective-permute-done.1), kind=kOutput, calls=%fused_computation.56 | convolution fusion | flops 805306368 | bytes 3145728 | tf_op jit(solution)/shard_map/dot_general | solution.py:41
  11.1 8.2 %collective-permute-done = f32[512,512]{1,0:T(8,128)} collective-permute-done((f32[512,512]{1,0:T(8,128)S(1)}, f32[512,512]{1,0:T(8,128)}, u32[]{:S(2)}, u32[]{:S(2)}) %collective-permute-start) | collective-permute-done | bytes 1048608 | tf_op jit(solution)/shard_map/ppermute | solution.py:33
  19.2 2.3 %convolution_add_fusion.5 = f32[512,512]{1,0:T(8,128)S(1)} fusion(f32[512,512]{1,0:T(8,128)S(1)} %fusion.23, f32[512,512]{1,0:T(8,128)S(1)} %get-tuple-element.7, f32[512,512]{1,0:T(8,128)} %collective-permute-done), kind=kOutput, calls=%fused_computation.18 | convolution fusion | flops 805568512 | bytes 4194304 | tf_op jit(solution)/shard_map/dot_general | solution.py:41
  21.5 1.0 fusion.24
  22.5 1.0 convolution_add_fusion.4
  23.6 1.9 fusion.26
  25.4 1.9 fusion.25
  27.3 4.6 %collective-permute-done.2 = f32[576,512]{1,0:T(8,128)} collective-permute-done((f32[576,512]{1,0:T(8,128)}, f32[576,512]{1,0:T(8,128)}, u32[]{:S(2)}, u32[]{:S(2)}) %collective-permute-start.2) | collective-permute-done | bytes 1179680 | tf_op jit(solution)/shard_map/ppermute | solution.py:33
  31.8 2.2 %convolution_negate_fusion.5 = f32[512,512]{1,0:T(8,128)S(1)} fusion(f32[512,512]{1,0:T(8,128)S(1)} %fusion.25, f32[576,512]{1,0:T(8,128)} %collective-permute-done.2), kind=kOutput, calls=%fused_computation.16 | convolution fusion | flops 805568512 | bytes 3145728 | tf_op jit(solution)/shard_map/dot_general | solution.py:41
  34.1 1.8 collective-permute-start.5
  35.9 1.0 convolution_negate_fusion.4
  38.7 1.5 fusion
  40.5 4.1 %collective-permute-start.7 = (f32[576,512]{1,0:T(8,128)S(1)}, f32[576,512]{1,0:T(8,128)S(1)}, u32[]{:S(2)}, u32[]{:S(2)}) collective-permute-start(f32[576,512]{1,0:T(8,128)S(1)} %get-tuple-element.10), channel_id=1, source_target_pairs={{0,126},{1,3},{2,0},{3,5},{4,2},{5,7},{6,4},{7,9},{8,6},{9,11},{10... | collective-permute-start | bytes 3538952 | tf_op jit(solution)/shard_map/ppermute | solution.py:33
  44.6 15.2 %collective-permute-done.5 = f32[512,512]{1,0:T(8,128)S(1)} collective-permute-done((f32[512,512]{1,0:T(8,128)S(1)}, f32[512,512]{1,0:T(8,128)S(1)}, u32[]{:S(2)}, u32[]{:S(2)}) %collective-permute-start.5) | collective-permute-done | bytes 1048608 | tf_op jit(solution)/shard_map/ppermute | solution.py:33
  59.9 1.0 fusion.27
  60.9 4.4 %collective-permute-done.4 = f32[512,512]{1,0:T(8,128)S(1)} collective-permute-done((f32[512,512]{1,0:T(8,128)S(1)}, f32[512,512]{1,0:T(8,128)S(1)}, u32[]{:S(2)}, u32[]{:S(2)}) %collective-permute-start.4) | collective-permute-done | bytes 1048608 | tf_op jit(solution)/shard_map/ppermute | solution.py:33
  65.4 1.1 convolution_add_fusion.3
  66.4 1.0 fusion.28
  67.5 1.0 convolution_add_fusion.2
  69.2 1.9 fusion.29
  71.0 1.9 fusion.30
  72.9 12.2 %collective-permute-done.7 = f32[576,512]{1,0:T(8,128)S(1)} collective-permute-done((f32[576,512]{1,0:T(8,128)S(1)}, f32[576,512]{1,0:T(8,128)S(1)}, u32[]{:S(2)}, u32[]{:S(2)}) %collective-permute-start.7) | collective-permute-done | bytes 1179680 | tf_op jit(solution)/shard_map/ppermute | solution.py:33
  85.1 1.0 convolution_negate_fusion.2
  86.2 0.8 collective-permute-done.6
  87.0 1.1 broadcast_select_fusion.1
  88.1 3.6 %collective-permute-start.10 = (f32[512,512]{1,0:T(8,128)S(1)}, f32[512,512]{1,0:T(8,128)S(1)}, u32[]{:S(2)}, u32[]{:S(2)}) collective-permute-start(f32[512,512]{1,0:T(8,128)S(1)} %get-tuple-element.6), channel_id=1, source_target_pairs={{0,2},{1,36},{2,39},{3,1},{4,3},{5,37},{6,38},{7,0},{8,13},{9,43},... | collective-permute-start | bytes 3145736 | tf_op jit(solution)/shard_map/ppermute | solution.py:33
  93.1 1.9 collective-permute-start.8
  95.0 9.2 %collective-permute-done.10 = f32[512,512]{1,0:T(8,128)S(1)} collective-permute-done((f32[512,512]{1,0:T(8,128)S(1)}, f32[512,512]{1,0:T(8,128)S(1)}, u32[]{:S(2)}, u32[]{:S(2)}) %collective-permute-start.10) | collective-permute-done | bytes 1048608 | tf_op jit(solution)/shard_map/ppermute | solution.py:33
  104.7 12.1 %collective-permute-done.8 = f32[576,512]{1,0:T(8,128)S(1)} collective-permute-done((f32[576,512]{1,0:T(8,128)S(1)}, f32[576,512]{1,0:T(8,128)S(1)}, u32[]{:S(2)}, u32[]{:S(2)}) %collective-permute-start.8) | collective-permute-done | bytes 1179680 | tf_op jit(solution)/shard_map/ppermute | solution.py:33
  117.4 1.2 collective-permute-start.12
  118.6 4.6 %collective-permute-start.14 = (f32[576,512]{1,0:T(8,128)S(1)}, f32[576,512]{1,0:T(8,128)S(1)}, u32[]{:S(2)}, u32[]{:S(2)}) collective-permute-start(f32[576,512]{1,0:T(8,128)S(1)} %collective-permute-done.8), channel_id=1, source_target_pairs={{2,3},{36,37},{39,38},{1,0},{3,2},{37,36},{38,39},{0,1},{13,12},{4... | collective-permute-start | bytes 3538952 | tf_op jit(solution)/shard_map/ppermute | solution.py:33
  123.2 1.0 fusion.32
  124.2 8.2 %collective-permute-done.9 = f32[576,512]{1,0:T(8,128)S(1)} collective-permute-done((f32[576,512]{1,0:T(8,128)S(1)}, f32[576,512]{1,0:T(8,128)S(1)}, u32[]{:S(2)}, u32[]{:S(2)}) %collective-permute-start.9) | collective-permute-done | bytes 1179680 | tf_op jit(solution)/shard_map/ppermute | solution.py:33
  132.5 1.1 convolution_add_fusion.1
  133.5 1.0 fusion.33
  134.6 1.0 convolution_add_fusion
  135.6 1.0 fusion.10
  136.7 7.0 %collective-permute-done.12 = f32[512,512]{1,0:T(8,128)S(1)} collective-permute-done((f32[512,512]{1,0:T(8,128)S(1)}, f32[512,512]{1,0:T(8,128)S(1)}, u32[]{:S(2)}, u32[]{:S(2)}) %collective-permute-start.12) | collective-permute-done | bytes 1048608 | tf_op jit(solution)/shard_map/ppermute | solution.py:33
  143.7 1.0 convolution_negate_fusion.1
  144.7 3.4 %collective-permute-start.13 = (f32[512,512]{1,0:T(8,128)S(1)}, f32[512,512]{1,0:T(8,128)S(1)}, u32[]{:S(2)}, u32[]{:S(2)}) collective-permute-start(f32[512,512]{1,0:T(8,128)S(1)} %convolution_negate_fusion.1), channel_id=1, source_target_pairs={{2,0},{36,16},{39,32},{1,48},{3,64},{37,80},{38,96},{0,112},{13,1}... | collective-permute-start | bytes 3145736 | tf_op jit(solution)/shard_map/ppermute | solution.py:33
  148.2 1.0 fusion.34
  149.2 2.0 convolution_negate_fusion
  151.3 1.5 collective-permute-start.15
  154.7 52.4 %collective-permute-done.16 = f32[64,512]{1,0:T(8,128)S(1)} collective-permute-done((f32[64,512]{1,0:T(8,128)S(1)}, f32[64,512]{1,0:T(8,128)S(1)}, u32[]{:S(2)}, u32[]{:S(2)}) %collective-permute-start.16) | collective-permute-done | bytes 131104 | tf_op jit(solution)/shard_map/ppermute | solution.py:33
  207.1 1.6 multiply_bitcast_fusion
  (27 shorter events, 8.4 us)
Async XLA Ops:
  0.6 6.0 %copy-start = (f32[1,64,512]{2,1,0:T(8,128)S(1)}, f32[1,64,512]{2,1,0:T(8,128)}, u32[]{:S(2)}) copy-start(f32[1,64,512]{2,1,0:T(8,128)} %param.5) | copy-start | bytes 393220
  2.5 6.3 %collective-permute-start.1 = (f32[512,512]{1,0:T(8,128)S(1)}, f32[512,512]{1,0:T(8,128)}, u32[]{:S(2)}, u32[]{:S(2)}) collective-permute-start(f32[512,512]{1,0:T(8,128)S(1)} %get-tuple-element.8), channel_id=1, source_target_pairs={{0,1},{1,0},{2,3},{3,2},{4,5},{5,4},{6,7},{7,6},{8,9},{9,8},{10,11... | collective-permute-start | bytes 3145736 | tf_op jit(solution)/shard_map/ppermute | solution.py:33
  2.6 16.6 %collective-permute-start = (f32[512,512]{1,0:T(8,128)S(1)}, f32[512,512]{1,0:T(8,128)}, u32[]{:S(2)}, u32[]{:S(2)}) collective-permute-start(f32[512,512]{1,0:T(8,128)S(1)} %get-tuple-element.7), channel_id=1, source_target_pairs={{0,127},{1,2},{2,1},{3,4},{4,3},{5,6},{6,5},{7,8},{8,7},{9,10},{10... | collective-permute-start | bytes 3145736 | tf_op jit(solution)/shard_map/ppermute | solution.py:33
  8.3 27.6 %collective-permute-start.3 = (f32[576,512]{1,0:T(8,128)}, f32[576,512]{1,0:T(8,128)S(1)}, u32[]{:S(2)}, u32[]{:S(2)}) collective-permute-start(f32[576,512]{1,0:T(8,128)} %get-tuple-element.12), channel_id=1, source_target_pairs={{0,1},{1,0},{2,3},{3,2},{4,5},{5,4},{6,7},{7,6},{8,9},{9,8},{10,11... | collective-permute-start | bytes 3538952 | tf_op jit(solution)/shard_map/ppermute | solution.py:33
  8.3 23.6 %collective-permute-start.2 = (f32[576,512]{1,0:T(8,128)}, f32[576,512]{1,0:T(8,128)}, u32[]{:S(2)}, u32[]{:S(2)}) collective-permute-start(f32[576,512]{1,0:T(8,128)} %get-tuple-element.11), channel_id=1, source_target_pairs={{0,127},{1,2},{2,1},{3,4},{4,3},{5,6},{6,5},{7,8},{8,7},{9,10},{10... | collective-permute-start | bytes 3538952 | tf_op jit(solution)/shard_map/ppermute | solution.py:33
  34.1 25.8 %collective-permute-start.5 = (f32[512,512]{1,0:T(8,128)S(1)}, f32[512,512]{1,0:T(8,128)S(1)}, u32[]{:S(2)}, u32[]{:S(2)}) collective-permute-start(f32[512,512]{1,0:T(8,128)S(1)} %convolution_negate_fusion.5), channel_id=1, source_target_pairs={{0,126},{1,3},{2,0},{3,5},{4,2},{5,7},{6,4},{7,9},{8,6},{9,11},{10... | collective-permute-start | bytes 3145736 | tf_op jit(solution)/shard_map/ppermute | solution.py:33
  36.9 28.5 %collective-permute-start.4 = (f32[512,512]{1,0:T(8,128)S(1)}, f32[512,512]{1,0:T(8,128)S(1)}, u32[]{:S(2)}, u32[]{:S(2)}) collective-permute-start(f32[512,512]{1,0:T(8,128)S(1)} %convolution_negate_fusion.4), channel_id=1, source_target_pairs={{0,2},{1,127},{2,4},{3,1},{4,6},{5,3},{6,8},{7,5},{8,10},{9,7},{10... | collective-permute-start | bytes 3145736 | tf_op jit(solution)/shard_map/ppermute | solution.py:33
  40.4 46.6 %collective-permute-start.6 = (f32[576,512]{1,0:T(8,128)S(1)}, f32[576,512]{1,0:T(8,128)S(1)}, u32[]{:S(2)}, u32[]{:S(2)}) collective-permute-start(f32[576,512]{1,0:T(8,128)S(1)} %get-tuple-element.9), channel_id=1, source_target_pairs={{0,2},{1,127},{2,4},{3,1},{4,6},{5,3},{6,8},{7,5},{8,10},{9,7},{10... | collective-permute-start | bytes 3538952 | tf_op jit(solution)/shard_map/ppermute | solution.py:33
  40.5 44.6 %collective-permute-start.7 = (f32[576,512]{1,0:T(8,128)S(1)}, f32[576,512]{1,0:T(8,128)S(1)}, u32[]{:S(2)}, u32[]{:S(2)}) collective-permute-start(f32[576,512]{1,0:T(8,128)S(1)} %get-tuple-element.10), channel_id=1, source_target_pairs={{0,126},{1,3},{2,0},{3,5},{4,2},{5,7},{6,4},{7,9},{8,6},{9,11},{10... | collective-permute-start | bytes 3538952 | tf_op jit(solution)/shard_map/ppermute | solution.py:33
  88.1 16.1 %collective-permute-start.10 = (f32[512,512]{1,0:T(8,128)S(1)}, f32[512,512]{1,0:T(8,128)S(1)}, u32[]{:S(2)}, u32[]{:S(2)}) collective-permute-start(f32[512,512]{1,0:T(8,128)S(1)} %get-tuple-element.6), channel_id=1, source_target_pairs={{0,2},{1,36},{2,39},{3,1},{4,3},{5,37},{6,38},{7,0},{8,13},{9,43},... | collective-permute-start | bytes 3145736 | tf_op jit(solution)/shard_map/ppermute | solution.py:33
  93.1 23.8 %collective-permute-start.8 = (f32[576,512]{1,0:T(8,128)S(1)}, f32[576,512]{1,0:T(8,128)S(1)}, u32[]{:S(2)}, u32[]{:S(2)}) collective-permute-start(f32[576,512]{1,0:T(8,128)S(1)} %pad_maximum_fusion.4), channel_id=1, source_target_pairs={{0,2},{1,36},{2,39},{3,1},{4,3},{5,37},{6,38},{7,0},{8,13},{9,43},... | collective-permute-start | bytes 3538952 | tf_op jit(solution)/shard_map/ppermute | solution.py:33
  104.2 19.0 %collective-permute-start.11 = (f32[512,512]{1,0:T(8,128)S(1)}, f32[512,512]{1,0:T(8,128)S(1)}, u32[]{:S(2)}, u32[]{:S(2)}) collective-permute-start(f32[512,512]{1,0:T(8,128)S(1)} %collective-permute-done.10), channel_id=1, source_target_pairs={{2,3},{36,37},{39,38},{1,0},{3,2},{37,36},{38,39},{0,1},{13,12},{4... | collective-permute-start | bytes 3145736 | tf_op jit(solution)/shard_map/ppermute | solution.py:33
  116.8 15.6 %collective-permute-start.9 = (f32[576,512]{1,0:T(8,128)S(1)}, f32[576,512]{1,0:T(8,128)S(1)}, u32[]{:S(2)}, u32[]{:S(2)}) collective-permute-start(f32[576,512]{1,0:T(8,128)S(1)} %collective-permute-done.8), channel_id=1, source_target_pairs={{2,122},{36,92},{39,95},{1,121},{3,13},{37,43},{38,40},{0,14},{13,... | collective-permute-start | bytes 3538952 | tf_op jit(solution)/shard_map/ppermute | solution.py:33
  117.4 26.3 %collective-permute-start.12 = (f32[512,512]{1,0:T(8,128)S(1)}, f32[512,512]{1,0:T(8,128)S(1)}, u32[]{:S(2)}, u32[]{:S(2)}) collective-permute-start(f32[512,512]{1,0:T(8,128)S(1)} %collective-permute-done.10), channel_id=1, source_target_pairs={{2,122},{36,92},{39,95},{1,121},{3,13},{37,43},{38,40},{0,14},{13,... | collective-permute-start | bytes 3145736 | tf_op jit(solution)/shard_map/ppermute | solution.py:33
  118.6 30.6 %collective-permute-start.14 = (f32[576,512]{1,0:T(8,128)S(1)}, f32[576,512]{1,0:T(8,128)S(1)}, u32[]{:S(2)}, u32[]{:S(2)}) collective-permute-start(f32[576,512]{1,0:T(8,128)S(1)} %collective-permute-done.8), channel_id=1, source_target_pairs={{2,3},{36,37},{39,38},{1,0},{3,2},{37,36},{38,39},{0,1},{13,12},{4... | collective-permute-start | bytes 3538952 | tf_op jit(solution)/shard_map/ppermute | solution.py:33
  144.7 62.3 %collective-permute-start.13 = (f32[512,512]{1,0:T(8,128)S(1)}, f32[512,512]{1,0:T(8,128)S(1)}, u32[]{:S(2)}, u32[]{:S(2)}) collective-permute-start(f32[512,512]{1,0:T(8,128)S(1)} %convolution_negate_fusion.1), channel_id=1, source_target_pairs={{2,0},{36,16},{39,32},{1,48},{3,64},{37,80},{38,96},{0,112},{13,1}... | collective-permute-start | bytes 3145736 | tf_op jit(solution)/shard_map/ppermute | solution.py:33
  151.3 55.8 %collective-permute-start.15 = (f32[512,512]{1,0:T(8,128)}, f32[512,512]{1,0:T(8,128)S(1)}, u32[]{:S(2)}, u32[]{:S(2)}) collective-permute-start(f32[512,512]{1,0:T(8,128)} %convolution_negate_fusion), channel_id=1, source_target_pairs={{2,0},{36,16},{39,32},{1,48},{3,64},{37,80},{38,96},{0,112},{13,1}... | collective-permute-start | bytes 3145736 | tf_op jit(solution)/shard_map/ppermute | solution.py:33
  154.6 52.5 %collective-permute-start.16 = (f32[64,512]{1,0:T(8,128)S(1)}, f32[64,512]{1,0:T(8,128)S(1)}, u32[]{:S(2)}, u32[]{:S(2)}) collective-permute-start(f32[64,512]{1,0:T(8,128)S(1)} %convolution_subtract_fusion), channel_id=1, source_target_pairs={{2,0},{36,16},{39,32},{1,48},{3,64},{37,80},{38,96},{0,112},{13,1}... | collective-permute-start | bytes 393224 | tf_op jit(solution)/shard_map/ppermute | solution.py:33
